TPU v7x, 32 devices: a whole 2x2x4 slice. The times are simulated.
32 devices in a mesh: space: 16 (over z, x, core), mem: 2 (over y).
Axes of the slice: x: 2, y: 2, z: 4, core: 2. Of those that a mesh axis runs over, the one named last changes fastest.
Arguments:
- control: bfloat16 [16, 4096, 256], P('mem', 'space'), may hold values from -6 to 6
- perturbations: bfloat16 [16, 4096, 256], P('mem', 'space'), may hold values from -1.5 to 1.5
- innovation: float32 [4096, 256], P('space'), may hold values from -6 to 6
- error_weight: float32 [4096, 256], P('space'), may hold values from 0.3 to 3
Outputs:
- gradient: bfloat16 [16, 4096, 256], P('mem', 'space')
- increment: float32 [4096, 256], P('space', 'mem')
All inputs are finite; a program needn't handle non-finite values.
Results may differ from a plain program's by a relative error of at most 0.0067.
Values may be sent and summed in bfloat16 or wider, within the bound.
A program may use at most 64 MiB of HBM per device.

v0:
```python
import math

import jax
import jax.numpy as jnp
from jax import lax
from jax.sharding import PartitionSpec as P

BAND = 256
ROW_SCALE = 192
COL_SCALE = 1


def passed_along(value, axis, by):
    size = lax.axis_size(axis)
    pairs = [(i, i + by) for i in range(size) if 0 <= i + by < size]
    return lax.ppermute(value, axis, pairs)


def column_table(count):
    place = jnp.arange(count, dtype=jnp.float32)
    gap = place[:, None] - place[None, :]
    taper_factor = (COL_SCALE * math.sqrt(math.pi)) ** (-0.5)
    return (taper_factor * jnp.exp(-gap * gap / (2.0 * COL_SCALE * COL_SCALE))).astype(jnp.bfloat16)


def row_table(count):
    inner = jnp.arange(count, dtype=jnp.float32)[:, None]
    outer = jnp.arange(count + 2 * BAND, dtype=jnp.float32)[None, :]
    gap = inner + BAND - outer
    taper_factor = (ROW_SCALE * math.sqrt(math.pi)) ** (-0.5)
    values = taper_factor * jnp.exp(-gap * gap / (2.0 * ROW_SCALE * ROW_SCALE))
    return jnp.where(jnp.abs(gap) <= BAND, values, 0.0).astype(jnp.bfloat16)


def extend(block):
    hop_index = 1
    upper = [passed_along(block, "space", hop_index)]
    hop_index = 1
    lower = [passed_along(block, "space", -hop_index)]
    return jnp.concatenate(upper + [block] + lower, axis=1)


def on_device(control, perturbations, innovation, error_weight):
    row_count = control.shape[1]
    col_count = control.shape[2]
    column_lookup = column_table(col_count)
    rows_table = row_table(row_count)

    def cols_filter(depth_field):
        return jnp.einsum(
            "gsy,yh->gsh", depth_field, column_lookup, preferred_element_type=jnp.float32
        ).astype(jnp.bfloat16)

    def rows_filter(extended):
        return jnp.einsum("rj,mjc->mrc", rows_table, extended, preferred_element_type=jnp.float32)

    extended = extend(cols_filter(control))
    localized = rows_filter(extended)
    member_terms = jnp.sum(perturbations.astype(jnp.float32) * localized, axis=0)
    share_cols = col_count // lax.axis_size("mem")
    offset_cols = lax.axis_index("mem") * share_cols
    increment_out = lax.psum_scatter(member_terms, "mem", scatter_dimension=1, tiled=True)
    weight_share = lax.dynamic_slice_in_dim(error_weight, offset_cols, share_cols, 1)
    innovation_portion = lax.dynamic_slice_in_dim(innovation, offset_cols, share_cols, 1)
    weighted_share = (weight_share * (increment_out - innovation_portion)).astype(jnp.bfloat16)
    weighted = lax.all_gather(weighted_share, "mem", axis=1, tiled=True)
    weighted = lax.optimization_barrier(weighted)
    product = (perturbations.astype(jnp.float32) * weighted.astype(jnp.float32)[None]).astype(
        jnp.bfloat16
    )
    adjoint_rim = extend(cols_filter(product))
    gradient = rows_filter(adjoint_rim).astype(jnp.bfloat16)
    return (gradient, increment_out)


def solution(mesh):
    placed = (P("mem", "space", None), P("mem", "space", None), P("space", None), P("space", None))
    return jax.shard_map(
        on_device,
        mesh=mesh,
        in_specs=placed,
        out_specs=(P("mem", "space", None), P("space", "mem")),
        check_vma=False,
    )
```

profile of v0, /device:TPU:1, one launch (start us, length us, event | category | flops | bytes accessed | tf_op | source)
XLA Modules:
  0.0 99.7 jit_solution(12562481666278942338)
XLA Ops:
  7.2 0.0 copy-start
  7.2 0.0 copy-start.1
  7.2 0.0 reduce-scatter.2.cloned.1.call-start
  7.2 1.2 %copy-done = bf16[8,256,256]{2,1,0:T(8,128)(2,1)S(1)} copy-done((bf16[8,256,256]{2,1,0:T(8,128)(2,1)S(1)}, bf16[8,256,256]{2,1,0:T(8,128)(2,1)}, u32[]{:S(2)}) %copy-start) | copy-done | bytes 1048600
  8.4 1.5 %fusion.19 = bf16[8,256,256]{2,1,0:T(8,128)(2,1)} fusion(bf16[8,256,256]{2,1,0:T(8,128)(2,1)S(1)} %copy-done), kind=kOutput, calls=%fused_computation.19 | convolution fusion | flops 269352960 | bytes 2097152 | tf_op jit(solution)/shard_map/gsy,yh->gsh/dot_general | solution.py:50
  9.9 4.5 %collective-permute-start = (bf16[8,256,256]{2,1,0:T(8,128)(2,1)}, bf16[8,256,256]{2,1,0:T(8,128)(2,1)}, u32[]{:S(2)}, u32[]{:S(2)}) collective-permute-start(bf16[8,256,256]{2,1,0:T(8,128)(2,1)} %fusion.19), channel_id=1, source_target_pairs={{0,2},{2,4},{4,6},{6,8},{8,10},{10,12},{12,14},{14,16},{16,18},{18... | collective-permute-start | bytes 3145736 | tf_op jit(solution)/shard_map/ppermute | solution.py:16
  14.4 1.9 %collective-permute-start.1 = (bf16[8,256,256]{2,1,0:T(8,128)(2,1)}, bf16[8,256,256]{2,1,0:T(8,128)(2,1)}, u32[]{:S(2)}, u32[]{:S(2)}) collective-permute-start(bf16[8,256,256]{2,1,0:T(8,128)(2,1)} %fusion.19), channel_id=1, source_target_pairs={{2,0},{4,2},{6,4},{8,6},{10,8},{12,10},{14,12},{16,14},{18,16},{20... | collective-permute-start | bytes 3145736 | tf_op jit(solution)/shard_map/ppermute | solution.py:16
  16.3 0.0 copy-done.1
  16.3 0.5 copy.12
  16.9 0.0 copy-start.3
  16.9 0.0 copy-start.4
  16.9 20.8 %collective-permute-done = bf16[8,256,256]{2,1,0:T(8,128)(2,1)} collective-permute-done((bf16[8,256,256]{2,1,0:T(8,128)(2,1)}, bf16[8,256,256]{2,1,0:T(8,128)(2,1)}, u32[]{:S(2)}, u32[]{:S(2)}) %collective-permute-start) | collective-permute-done | bytes 1048608 | tf_op jit(solution)/shard_map/ppermute | solution.py:16
  37.7 0.0 collective-permute-done.1
  37.7 3.8 %fusion.12 = f32[256,256]{0,1:T(8,128)} fusion(bf16[8,256,256]{1,2,0:T(8,128)(2,1)S(1)} %copy.12, bf16[8,256,256]{2,1,0:T(8,128)(2,1)} %collective-permute-done.1, bf16[8,256,256]{2,1,0:T(8,128)(2,1)} %fusion.19, bf16[8,256,256]{2,1,0:T(8,128)(2,1)} %collective-permute-done, f32[256]{0:T(256)S(1)} %iota_add_fusion), kind=kOutput, calls=%fused_computation.14 | convolution fusion | flops 818020352 | bytes 4457472 | tf_op jit(solution)/shard_map/rj,mjc->mrc/dot_general | solution.py:55
  41.5 0.0 reduce-scatter.2.cloned.1.call-update
  41.5 0.0 copy-done.3
  41.5 0.0 copy-done.4
  41.5 0.1 copy.23
  41.6 0.1 copy.24
  41.7 12.9 %reduce-scatter.2.cloned.1.call-done = f32[256,128]{0,1:T(8,128)} async-done(((f32[256,256]{0,1:T(8,128)}), f32[256,128]{0,1:T(8,128)}) %reduce-scatter.2.cloned.1.call-update) | async-done | bytes 131088 | tf_op jit(solution)/shard_map/reduce_scatter | solution.py:62
  54.7 0.9 multiply_convert_fusion
  55.6 3.8 %all_gather.3 = bf16[256,256]{0,1:T(8,128)(2,1)S(1)} all-gather(bf16[256,128]{0,1:T(8,128)(2,1)S(1)} %multiply_convert_fusion), channel_id=1, replica_groups=mesh['space'=16,'mem'=2] {'mem'}, dimensions={1}, use_global_device_ids=true | all-gather | bytes 196608 | tf_op jit(solution)/shard_map/all_gather | solution.py:66
  59.4 0.0 copy-start.2
  59.4 0.6 convolution_convert_fusion
  60.0 4.8 %collective-permute-start.2 = (bf16[8,256,256]{2,1,0:T(8,128)(2,1)S(1)}, bf16[8,256,256]{2,1,0:T(8,128)(2,1)S(1)}, u32[]{:S(2)}, u32[]{:S(2)}) collective-permute-start(bf16[8,256,256]{2,1,0:T(8,128)(2,1)S(1)} %convolution_convert_fusion), channel_id=1, source_target_pairs={{0,2},{2,4},{4,6},{6,8},{8,10},{10,12},{12,14},{14,16},{16,18},{18... | collective-permute-start | bytes 3145736 | tf_op jit(solution)/shard_map/ppermute | solution.py:16
  64.8 1.9 %collective-permute-start.3 = (bf16[8,256,256]{2,1,0:T(8,128)(2,1)S(1)}, bf16[8,256,256]{2,1,0:T(8,128)(2,1)}, u32[]{:S(2)}, u32[]{:S(2)}) collective-permute-start(bf16[8,256,256]{2,1,0:T(8,128)(2,1)S(1)} %convolution_convert_fusion), channel_id=1, source_target_pairs={{2,0},{4,2},{6,4},{8,6},{10,8},{12,10},{14,12},{16,14},{18,16},{20... | collective-permute-start | bytes 3145736 | tf_op jit(solution)/shard_map/ppermute | solution.py:16
  66.8 0.0 copy-done.2
  66.8 0.8 copy.19
  67.5 20.3 %collective-permute-done.2 = bf16[8,256,256]{2,1,0:T(8,128)(2,1)S(1)} collective-permute-done((bf16[8,256,256]{2,1,0:T(8,128)(2,1)S(1)}, bf16[8,256,256]{2,1,0:T(8,128)(2,1)S(1)}, u32[]{:S(2)}, u32[]{:S(2)}) %collective-permute-start.2) | collective-permute-done | bytes 1048608 | tf_op jit(solution)/shard_map/ppermute | solution.py:16
  87.8 0.0 copy-start.5
  87.8 1.0 copy-done.5
  88.8 0.0 collective-permute-done.3
  88.8 2.8 %fusion.20 = bf16[8,256,256]{1,2,0:T(8,128)(2,1)S(1)} fusion(bf16[8,256,256]{2,1,0:T(8,128)(2,1)} %collective-permute-done.3, bf16[8,256,256]{2,1,0:T(8,128)(2,1)S(1)} %convolution_convert_fusion, bf16[8,256,256]{2,1,0:T(8,128)(2,1)} %copy-done.5, f32[256]{0:T(256)S(1)} %iota_add_fusion), kind=kOutput, calls=%fused_computation.20 | convolution fusion | flops 817037312 | bytes 4195328 | tf_op jit(solution)/shard_map/rj,mjc->mrc/dot_general | solution.py:55
  91.5 1.3 %copy.18 = bf16[8,256,256]{2,1,0:T(8,128)(2,1)} copy(bf16[8,256,256]{1,2,0:T(8,128)(2,1)S(1)} %fusion.20) | data formatting | bytes 2097152
  (3 shorter events, 0.1 us)
Async XLA Ops:
  7.2 1.2 %copy-start = (bf16[8,256,256]{2,1,0:T(8,128)(2,1)S(1)}, bf16[8,256,256]{2,1,0:T(8,128)(2,1)}, u32[]{:S(2)}) copy-start(bf16[8,256,256]{2,1,0:T(8,128)(2,1)} %param.4) | copy-start | bytes 3145732
  7.2 9.1 %copy-start.1 = (bf16[8,256,256]{2,1,0:T(8,128)(2,1)S(1)}, bf16[8,256,256]{2,1,0:T(8,128)(2,1)}, u32[]{:S(2)}) copy-start(bf16[8,256,256]{2,1,0:T(8,128)(2,1)} %param.5) | copy-start | bytes 3145732
  7.2 47.5 %reduce-scatter.2.cloned.1.call-start = ((), (), s32[]{:S(2)}) async-start(), calls=%async_computation.1 | async-start | bytes 393216 | tf_op jit(solution)/shard_map/reduce_scatter | solution.py:62
  9.9 27.8 %collective-permute-start = (bf16[8,256,256]{2,1,0:T(8,128)(2,1)}, bf16[8,256,256]{2,1,0:T(8,128)(2,1)}, u32[]{:S(2)}, u32[]{:S(2)}) collective-permute-start(bf16[8,256,256]{2,1,0:T(8,128)(2,1)} %fusion.19), channel_id=1, source_target_pairs={{0,2},{2,4},{4,6},{6,8},{8,10},{10,12},{12,14},{14,16},{16,18},{18... | collective-permute-start | bytes 3145736 | tf_op jit(solution)/shard_map/ppermute | solution.py:16
  14.4 23.3 %collective-permute-start.1 = (bf16[8,256,256]{2,1,0:T(8,128)(2,1)}, bf16[8,256,256]{2,1,0:T(8,128)(2,1)}, u32[]{:S(2)}, u32[]{:S(2)}) collective-permute-start(bf16[8,256,256]{2,1,0:T(8,128)(2,1)} %fusion.19), channel_id=1, source_target_pairs={{2,0},{4,2},{6,4},{8,6},{10,8},{12,10},{14,12},{16,14},{18,16},{20... | collective-permute-start | bytes 3145736 | tf_op jit(solution)/shard_map/ppermute | solution.py:16
  16.9 24.6 %copy-start.3 = (f32[256,256]{1,0:T(8,128)S(1)}, f32[256,256]{1,0:T(8,128)}, u32[]{:S(2)}) copy-start(f32[256,256]{1,0:T(8,128)} %param.6) | copy-start | bytes 786436
  16.9 24.6 %copy-start.4 = (f32[256,256]{1,0:T(8,128)S(1)}, f32[256,256]{1,0:T(8,128)}, u32[]{:S(2)}) copy-start(f32[256,256]{1,0:T(8,128)} %param.7) | copy-start | bytes 786436
  59.4 7.3 %copy-start.2 = (f32[256,128]{0,1:T(8,128)S(1)}, f32[256,128]{0,1:T(8,128)}, u32[]{:S(2)}) copy-start(f32[256,128]{0,1:T(8,128)} %reduce-scatter.2.cloned.1.call-done) | copy-start | bytes 393220
  60.0 27.8 %collective-permute-start.2 = (bf16[8,256,256]{2,1,0:T(8,128)(2,1)S(1)}, bf16[8,256,256]{2,1,0:T(8,128)(2,1)S(1)}, u32[]{:S(2)}, u32[]{:S(2)}) collective-permute-start(bf16[8,256,256]{2,1,0:T(8,128)(2,1)S(1)} %convolution_convert_fusion), channel_id=1, source_target_pairs={{0,2},{2,4},{4,6},{6,8},{8,10},{10,12},{12,14},{14,16},{16,18},{18... | collective-permute-start | bytes 3145736 | tf_op jit(solution)/shard_map/ppermute | solution.py:16
  64.8 23.9 %collective-permute-start.3 = (bf16[8,256,256]{2,1,0:T(8,128)(2,1)S(1)}, bf16[8,256,256]{2,1,0:T(8,128)(2,1)}, u32[]{:S(2)}, u32[]{:S(2)}) collective-permute-start(bf16[8,256,256]{2,1,0:T(8,128)(2,1)S(1)} %convolution_convert_fusion), channel_id=1, source_target_pairs={{2,0},{4,2},{6,4},{8,6},{10,8},{12,10},{14,12},{16,14},{18,16},{20... | collective-permute-start | bytes 3145736 | tf_op jit(solution)/shard_map/ppermute | solution.py:16
  87.8 1.0 copy-start.5
Sparse Core Ops, SparseCore 0:
  41.6 13.0 reduce-scatter.1
where the time goes:
time: 100 us; the launch traced here: 99.7 us
  waiting for transfers between devices  54 us (54%)
  between operations  14.2 us (14%)
  starting transfers between devices  13.2 us (13%)
  matrix products  8.6 us (9%)
  local copies, waits for them, and re-layouts  4.96 us (5%)
  blocking collectives  3.79 us (4%)
    ppermute x4, waiting for transfers between devices, passed_along(): return lax.ppermute(value, axis, pairs)  41 us
    ppermute x4, starting transfers between devices, passed_along(): return lax.ppermute(value, axis, pairs)  13.2 us
    reduce_scatter x1, waiting for transfers between devices, on_device(): lax.psum_scatter(member_terms, 'mem', scatter_dimension=1, tiled=True)  12.9 us
    dot_general x2, matrix products, rows_filter(): jnp.einsum('rj,mjc->mrc', rows_table, extended, preferred_element_type=jn...  6.56 us
    unnamed x17, local copies, waits for them, and re-layouts  4.94 us
    all_gather x1, blocking collectives, on_device(): weighted = lax.all_gather(weighted_share, 'mem', axis=1, tiled=True)  3.79 us
    dot_general x2, matrix products, cols_filter(): jnp.einsum('gsy,yh->gsh', depth_field, column_lookup, preferred_element_t...  2.04 us
  transfers between devices with their start and end apart: 5, of which 3 were waited for; matrix products, arithmetic and copies ran while one was open for 2% of the time, Pallas kernels for 0%

commit v1 on v0

v1 whole, which is shorter than its diff:
```python
import functools
import math

import jax
import jax.numpy as jnp
from jax import lax
from jax.experimental import pallas as pl
from jax.experimental.pallas import tpu as pltpu
from jax.sharding import PartitionSpec as P

BAND = 256
ROW_SCALE = 192
COL_SCALE = 1
CHUNKS = 2
TILE = 16
MESH = pl.DeviceIdType.MESH


def taper(gap, scale):
    factor = (scale * math.sqrt(math.pi)) ** (-0.5)
    return factor * jnp.exp(-gap * gap / (2.0 * scale * scale))


def dot(a, b):
    return jnp.dot(a, b, preferred_element_type=jnp.float32)


def kernel(
    space_size, mem_size, share,
    control, pert, innovation, error_weight, gradient, increment,
    own_control, own_pert, own_innovation, own_weight,
    halo, local, centre, term_out, term_in, weighted, total, columns, result,
    col_table, row_table,
    load_sem, halo_send, halo_recv, term_send, term_recv,
    weight_send, weight_recv, inc_send, inc_recv, out_sem,
):
    members, rows, cols = control.shape
    step = rows // CHUNKS
    part = step // mem_size
    i = lax.axis_index("space")
    m = lax.axis_index("mem")
    has = {-1: i > 0, 1: i < space_size - 1}
    peers = [(db, dm) for db in (-1, 0, 1) for dm in range(mem_size) if (db, dm) != (0, 0)]

    def when(db, action):
        if db == 0:
            action()
        else:
            pl.when(has[db])(action)

    def device(db, dm):
        return {"space": i + db, "mem": lax.rem(m + dm + mem_size, mem_size)}

    def slot(db, dm):
        return (db + 1) * mem_size + dm

    def owned(chunk, owner):
        return pl.ds(pl.multiple_of(chunk * step + owner * part, part), part)

    def remote(src, dst, send, recv, target):
        return pltpu.make_async_remote_copy(
            src_ref=src, dst_ref=dst, send_sem=send, recv_sem=recv,
            device_id=target, device_id_type=MESH,
        )

    def halo_copy(db, chunk, target):
        side = 0 if db == 1 else 1
        span = pl.ds(chunk * step, step)
        return remote(
            pert.at[:, span, :], halo.at[side, :, span, :],
            halo_send.at[side, chunk], halo_recv.at[side, chunk], target,
        )

    def term_copy(db, dm, chunk, target):
        place = slot(db, dm)
        return remote(
            term_out.at[db + 1, owned(chunk, lax.rem(m + dm, mem_size)), :],
            term_in.at[chunk, place],
            term_send.at[chunk, place], term_recv.at[chunk, place], target,
        )

    def weight_copy(db, dm, chunk, owner, target):
        place = slot(db, dm)
        return remote(
            weighted.at[1, owned(chunk, owner), :], weighted.at[1 - db, owned(chunk, owner), :],
            weight_send.at[chunk, place], weight_recv.at[chunk, place], target,
        )

    def inc_copy(dm, chunk, owner, target):
        return remote(
            total.at[owned(chunk, owner), :], total.at[owned(chunk, owner), :],
            inc_send.at[chunk, dm], inc_recv.at[chunk, dm], target,
        )

    loads = [
        pltpu.make_async_copy(src, dst, load_sem.at[n])
        for n, (src, dst) in enumerate((
            (control, own_control), (pert, own_pert),
            (innovation, own_innovation), (error_weight, own_weight),
        ))
    ]
    for load in loads:
        load.start()

    barrier = pltpu.get_barrier_semaphore()
    for db, dm in peers:
        def greet(db=db, dm=dm):
            pl.semaphore_signal(barrier, inc=1, device_id=device(db, dm), device_id_type=MESH)
        when(db, greet)
    sides = has[-1].astype(jnp.int32) + has[1].astype(jnp.int32)
    pl.semaphore_wait(barrier, mem_size - 1 + mem_size * sides)

    for chunk in range(CHUNKS):
        for db in (1, -1):
            when(db, lambda db=db, chunk=chunk: halo_copy(db, chunk, device(db, 0)).start())

    for db in (-1, 1):
        def clear(db=db):
            side = 0 if db == -1 else 1
            halo[side] = jnp.zeros(halo.shape[1:], halo.dtype)
            weighted[1 + db] = jnp.zeros((rows, cols), weighted.dtype)
            for dm in range(mem_size):
                for chunk in range(CHUNKS):
                    term_in[chunk, slot(-db, dm)] = jnp.zeros((part, cols), term_in.dtype)
        pl.when(jnp.logical_not(has[db]))(clear)

    inner = lax.broadcasted_iota(jnp.int32, (rows, rows), 0).astype(jnp.float32)
    outer = lax.broadcasted_iota(jnp.int32, (rows, rows), 1).astype(jnp.float32)
    for block in range(3):
        gap = inner - outer + BAND * (1 - block)
        values = jnp.where(jnp.abs(gap) <= BAND, taper(gap, ROW_SCALE), 0.0)
        row_table[:, block * rows:(block + 1) * rows] = values.astype(jnp.bfloat16)
    place = lax.broadcasted_iota(jnp.int32, (cols, cols), 0).astype(jnp.float32)
    other = lax.broadcasted_iota(jnp.int32, (cols, cols), 1).astype(jnp.float32)
    col_table[...] = taper(place - other, COL_SCALE).astype(jnp.bfloat16)
    centre[...] = jnp.zeros_like(centre)

    for load in loads:
        load.wait()

    def forward(k, carry):
        smoothed = dot(own_control[k], col_table[...]).astype(jnp.bfloat16)
        local[0, k] = dot(row_table[:, 2 * rows:], smoothed)
        local[1, k] = dot(row_table[:, :rows], smoothed)
        centre[...] += own_pert[k].astype(jnp.float32) * dot(row_table[:, rows:2 * rows], smoothed)
        return carry

    lax.fori_loop(0, members, forward, 0)
    term_out[1] = centre[...].astype(jnp.bfloat16)
    for chunk in range(CHUNKS):
        for dm in range(1, mem_size):
            term_copy(0, dm, chunk, device(0, dm)).start()

    def send_terms(chunk):
        for db in (-1, 1):
            def terms(db=db):
                side = 0 if db == -1 else 1
                halo_copy(-db, chunk, device(db, 0)).wait_recv()

                def tile(t, carry):
                    span = pl.ds(pl.multiple_of(chunk * step + t * TILE, TILE), TILE)
                    acc = jnp.zeros((TILE, cols), jnp.float32)
                    for k in range(members):
                        acc += halo[side, k, span, :].astype(jnp.float32) * local[side, k, span, :]
                    term_out[db + 1, span, :] = acc.astype(jnp.bfloat16)
                    return carry

                lax.fori_loop(0, step // TILE, tile, 0)
                for dm in range(mem_size):
                    term_copy(db, dm, chunk, device(db, dm)).start()
            when(db, terms)

    def send_weighted(chunk):
        for db, dm in peers:
            when(-db, lambda db=db, dm=dm: term_copy(db, dm, chunk, device(-db, -dm)).wait_recv())
        span = owned(chunk, m)
        sums = centre[span, :]
        for db, dm in peers:
            sums += term_in[chunk, slot(db, dm)].astype(jnp.float32)
        total[span, :] = sums
        weighted[1, span, :] = (
            own_weight[span, :] * (sums - own_innovation[span, :])
        ).astype(jnp.bfloat16)
        for db, dm in peers:
            when(db, lambda db=db, dm=dm: weight_copy(db, dm, chunk, m, device(db, dm)).start())
        for dm in range(1, mem_size):
            inc_copy(dm, chunk, m, device(0, dm)).start()

    def adjoint_cols(chunk):
        for db, dm in peers:
            owner = lax.rem(m - dm + mem_size, mem_size)
            when(-db, lambda db=db, dm=dm, owner=owner: weight_copy(
                db, dm, chunk, owner, device(-db, -dm)).wait_recv())
        span = pl.ds(chunk * step, step)

        def member(k, carry):
            fields = (halo[0, k, span, :], own_pert[k, span, :], halo[1, k, span, :])
            for block, field in enumerate(fields):
                product = field * weighted[block, span, :]
                columns[k, pl.ds(block * rows + chunk * step, step), :] = dot(
                    product, col_table[...]
                ).astype(jnp.bfloat16)
            return carry

        lax.fori_loop(0, members, member, 0)

    for turn in range(CHUNKS + 2):
        if turn < CHUNKS:
            send_terms(turn)
        if 0 <= turn - 1 < CHUNKS:
            send_weighted(turn - 1)
        if 0 <= turn - 2 < CHUNKS:
            adjoint_cols(turn - 2)

    def out_copy(k):
        return pltpu.make_async_copy(result.at[k], gradient.at[k], out_sem.at[k])

    def last(k, carry):
        result[k] = dot(row_table[...], columns[k]).astype(jnp.bfloat16)
        out_copy(k).start()
        return carry

    lax.fori_loop(0, members, last, 0)

    for chunk in range(CHUNKS):
        for dm in range(1, mem_size):
            owner = lax.rem(m - dm + mem_size, mem_size)
            inc_copy(dm, chunk, owner, device(0, -dm)).wait_recv()
    if increment.shape[1] == cols:
        view = total
    else:
        view = total.at[:, pl.ds(pl.multiple_of(m * share, share), share)]
    inc_out = pltpu.make_async_copy(view, increment, load_sem.at[0])
    inc_out.start()

    for chunk in range(CHUNKS):
        for db in (1, -1):
            when(db, lambda db=db, chunk=chunk: halo_copy(db, chunk, device(db, 0)).wait_send())
        for db, dm in peers:
            def sent(db=db, dm=dm, chunk=chunk):
                term_copy(db, dm, chunk, device(db, dm)).wait_send()
                weight_copy(db, dm, chunk, m, device(db, dm)).wait_send()
            when(db, sent)
        for dm in range(1, mem_size):
            inc_copy(dm, chunk, m, device(0, dm)).wait_send()
    for k in range(members):
        out_copy(k).wait()
    inc_out.wait()


def on_device(control, perturbations, innovation, error_weight):
    members, rows, cols = control.shape
    space_size = lax.axis_size("space")
    mem_size = lax.axis_size("mem")
    share = cols // mem_size
    aligned = share % 128 == 0
    part = rows // CHUNKS // mem_size
    slots = 3 * mem_size
    bf16, f32 = jnp.bfloat16, jnp.float32
    dma = pltpu.SemaphoreType.DMA
    gradient, increment = pl.pallas_call(
        functools.partial(kernel, space_size, mem_size, share),
        out_shape=(
            jax.ShapeDtypeStruct((members, rows, cols), bf16),
            jax.ShapeDtypeStruct((rows, share if aligned else cols), f32),
        ),
        in_specs=[pl.BlockSpec(memory_space=pl.ANY)] * 4,
        out_specs=(pl.BlockSpec(memory_space=pl.ANY),) * 2,
        scratch_shapes=[
            pltpu.VMEM((members, rows, cols), bf16),
            pltpu.VMEM((members, rows, cols), bf16),
            pltpu.VMEM((rows, cols), f32),
            pltpu.VMEM((rows, cols), f32),
            pltpu.VMEM((2, members, rows, cols), bf16),
            pltpu.VMEM((2, members, rows, cols), f32),
            pltpu.VMEM((rows, cols), f32),
            pltpu.VMEM((3, rows, cols), bf16),
            pltpu.VMEM((CHUNKS, slots, part, cols), bf16),
            pltpu.VMEM((3, rows, cols), bf16),
            pltpu.VMEM((rows, cols), f32),
            pltpu.VMEM((members, 3 * rows, cols), bf16),
            pltpu.VMEM((members, rows, cols), bf16),
            pltpu.VMEM((cols, cols), bf16),
            pltpu.VMEM((rows, 3 * rows), bf16),
            dma((4,)),
            dma((2, CHUNKS)),
            dma((2, CHUNKS)),
            dma((CHUNKS, slots)),
            dma((CHUNKS, slots)),
            dma((CHUNKS, slots)),
            dma((CHUNKS, slots)),
            dma((CHUNKS, mem_size)),
            dma((CHUNKS, mem_size)),
            dma((members,)),
        ],
        compiler_params=pltpu.CompilerParams(
            collective_id=0, has_side_effects=True, vmem_limit_bytes=40 * 1024 * 1024
        ),
    )(control, perturbations, innovation, error_weight)
    if not aligned:
        increment = lax.dynamic_slice_in_dim(increment, lax.axis_index("mem") * share, share, 1)
    return gradient, increment


def solution(mesh):
    placed = (P("mem", "space", None), P("mem", "space", None), P("space", None), P("space", None))
    return jax.shard_map(
        on_device,
        mesh=mesh,
        in_specs=placed,
        out_specs=(P("mem", "space", None), P("space", "mem")),
        check_vma=False,
    )
```

time: 100 us -> 50.2 us (0.50)
  waiting for transfers between devices: 54 us -> 0 us
  Pallas kernels: 0 us -> 43.3 us
  between operations: 14.2 us -> 0.65 us
  starting transfers between devices: 13.2 us -> 0 us
  matrix products: 8.6 us -> 0 us
  blocking collectives: 3.79 us -> 0 us
  local copies, waits for them, and re-layouts: 4.96 us -> 5.97 us
    pallas_call x0 -> x1, Pallas kernels: none -> 43.3 us  [on_device(): pl.pallas_call(functools.partial(kernel, space_size, mem_size, share), ou...]
    ppermute x4 -> x0, waiting for transfers between devices: 41 us -> none  [passed_along(): return lax.ppermute(value, axis, pairs)]
    ppermute x4 -> x0, starting transfers between devices: 13.2 us -> none  [passed_along(): return lax.ppermute(value, axis, pairs)]
    reduce_scatter x1 -> x0, waiting for transfers between devices: 12.9 us -> none  [on_device(): lax.psum_scatter(member_terms, 'mem', scatter_dimension=1, tiled=True)]
    dot_general x4 -> x0, matrix products: 8.6 us -> none  [the longest x2 6.56 us: rows_filter(): jnp.einsum('rj,mjc->mrc', rows_table, extended, preferred_element_type=jn...]
    all_gather x1 -> x0, blocking collectives: 3.79 us -> none  [on_device(): weighted = lax.all_gather(weighted_share, 'mem', axis=1, tiled=True)]
    unnamed x17 -> x10, local copies, waits for them, and re-layouts: 4.94 us -> 5.97 us
  transfers between devices with their start and end apart: 5 -> 0, of which waited for: 3 -> 0; matrix products, arithmetic and copies ran while one was open for 2% -> 0% of each run, Pallas kernels for 0% -> 0%
where the time goes in v1:
time: 50.2 us; the launch traced here: 50 us
  Pallas kernels  43.3 us (86%)
  local copies, waits for them, and re-layouts  5.97 us (12%)
  between operations  0.65 us (1%)
    pallas_call x1, Pallas kernels, on_device(): pl.pallas_call(functools.partial(kernel, space_size, mem_size, share), ou...  43.3 us
    unnamed x10, local copies, waits for them, and re-layouts  5.97 us

profile of v1, /device:TPU:1, one launch (start us, length us, event | category | flops | bytes accessed | tf_op | source)
XLA Modules:
  0.0 50.0 jit_solution(7104794523547847764)
XLA Ops:
  0.6 0.0 copy-start
  0.6 1.2 %copy-done = bf16[8,256,256]{2,1,0:T(8,128)(2,1)S(1)} copy-done((bf16[8,256,256]{2,1,0:T(8,128)(2,1)S(1)}, bf16[8,256,256]{2,1,0:T(8,128)(2,1)}, u32[]{:S(2)}) %copy-start) | copy-done | bytes 1048600
  1.9 0.0 copy-start.1
  1.9 1.2 %copy-done.1 = bf16[8,256,256]{2,1,0:T(8,128)(2,1)S(1)} copy-done((bf16[8,256,256]{2,1,0:T(8,128)(2,1)S(1)}, bf16[8,256,256]{2,1,0:T(8,128)(2,1)}, u32[]{:S(2)}) %copy-start.1) | copy-done | bytes 1048600
  3.1 0.0 copy-start.2
  3.1 0.9 %copy-done.2 = f32[256,256]{1,0:T(8,128)S(1)} copy-done((f32[256,256]{1,0:T(8,128)S(1)}, f32[256,256]{1,0:T(8,128)}, u32[]{:S(2)}) %copy-start.2) | copy-done | bytes 262168
  4.0 0.0 copy-start.3
  4.0 0.9 %copy-done.3 = f32[256,256]{1,0:T(8,128)S(1)} copy-done((f32[256,256]{1,0:T(8,128)S(1)}, f32[256,256]{1,0:T(8,128)}, u32[]{:S(2)}) %copy-start.3) | copy-done | bytes 262168
  5.0 43.3 %shard_map.59 = (bf16[8,256,256]{2,1,0:T(8,128)(2,1)S(1)}, f32[256,128]{1,0:T(8,128)S(1)}) custom-call(bf16[8,256,256]{2,1,0:T(8,128)(2,1)S(1)} %copy-done, bf16[8,256,256]{2,1,0:T(8,128)(2,1)S(1)} %copy-done.1, f32[256,256]{1,0:T(8,128)S(1)} %copy-done.2, f32[256,256]{1,0:T(8,128)S(1)} %copy-done.3), custom_call_target="tpu_custom_call" | custom-call | tf_op jit(solution)/shard_map/pallas_call | solution.py:261
  48.3 1.0 %copy.8 = bf16[8,256,256]{2,1,0:T(8,128)(2,1)} copy(bf16[8,256,256]{2,1,0:T(8,128)(2,1)S(1)} %get-tuple-element.4) | data formatting | bytes 2097152
  49.3 0.7 %copy.9 = f32[256,128]{1,0:T(8,128)} copy(f32[256,128]{1,0:T(8,128)S(1)} %get-tuple-element.5) | data formatting | bytes 262144
Async XLA Ops:
  0.6 1.2 %copy-start = (bf16[8,256,256]{2,1,0:T(8,128)(2,1)S(1)}, bf16[8,256,256]{2,1,0:T(8,128)(2,1)}, u32[]{:S(2)}) copy-start(bf16[8,256,256]{2,1,0:T(8,128)(2,1)} %control.1) | copy-start | bytes 3145732
  1.9 1.2 %copy-start.1 = (bf16[8,256,256]{2,1,0:T(8,128)(2,1)S(1)}, bf16[8,256,256]{2,1,0:T(8,128)(2,1)}, u32[]{:S(2)}) copy-start(bf16[8,256,256]{2,1,0:T(8,128)(2,1)} %pert.1) | copy-start | bytes 3145732
  3.1 0.9 %copy-start.2 = (f32[256,256]{1,0:T(8,128)S(1)}, f32[256,256]{1,0:T(8,128)}, u32[]{:S(2)}) copy-start(f32[256,256]{1,0:T(8,128)} %innovation.1) | copy-start | bytes 786436
  4.0 0.9 %copy-start.3 = (f32[256,256]{1,0:T(8,128)S(1)}, f32[256,256]{1,0:T(8,128)}, u32[]{:S(2)}) copy-start(f32[256,256]{1,0:T(8,128)} %error_weight.1) | copy-start | bytes 786436

commit v2 on v1

--- a/solution.py
+++ b/solution.py
@@ -11,8 +11,10 @@
 BAND = 256
 ROW_SCALE = 192
 COL_SCALE = 1
-CHUNKS = 2
+SIZES = (4, 4)
+CHUNKS = len(SIZES)
 TILE = 16
+UNROLL = 4
 MESH = pl.DeviceIdType.MESH
 
 
@@ -29,14 +31,15 @@
     space_size, mem_size, share,
     control, pert, innovation, error_weight, gradient, increment,
     own_control, own_pert, own_innovation, own_weight,
-    halo, local, centre, term_out, term_in, weighted, total, columns, result,
-    col_table, row_table,
-    load_sem, halo_send, halo_recv, term_send, term_recv,
-    weight_send, weight_recv, inc_send, inc_recv, out_sem,
+    halo, local, centre, term_out, term_in, weighted, total, result,
+    col_table, row_table, *rest,
 ):
+    tables, adjoints = rest[:CHUNKS], rest[CHUNKS:2 * CHUNKS]
+    (accumulated, load_sem, halo_send, halo_recv, term_send, term_recv,
+    weight_send, weight_recv, inc_send, inc_recv, out_sem) = rest[2 * CHUNKS:]
     members, rows, cols = control.shape
-    step = rows // CHUNKS
-    part = step // mem_size
+    steps = [rows * size // 8 for size in SIZES]
+    starts = [sum(steps[:n]) for n in range(CHUNKS)]
     i = lax.axis_index("space")
     m = lax.axis_index("mem")
     has = {-1: i > 0, 1: i < space_size - 1}
@@ -54,8 +57,23 @@
     def slot(db, dm):
         return (db + 1) * mem_size + dm
 
+    aligned = share % 128 == 0
+    inc_peers = [] if aligned else list(range(1, mem_size))
+
     def owned(chunk, owner):
-        return pl.ds(pl.multiple_of(chunk * step + owner * part, part), part)
+        if aligned:
+            return rows_of(chunk), pl.ds(pl.multiple_of(owner * share, share), share)
+        part = steps[chunk] // mem_size
+        first = starts[chunk] + owner * part
+        return pl.ds(pl.multiple_of(first, math.gcd(starts[chunk], part)), part), slice(None)
+
+    def rows_of(chunk):
+        return pl.ds(starts[chunk], steps[chunk])
+
+    def terms_of(chunk, place):
+        if aligned:
+            return place, rows_of(chunk), slice(None)
+        return place, pl.ds(starts[chunk] // mem_size, steps[chunk] // mem_size), slice(None)
 
     def remote(src, dst, send, recv, target):
         return pltpu.make_async_remote_copy(
@@ -65,7 +83,7 @@
 
     def halo_copy(db, chunk, target):
         side = 0 if db == 1 else 1
-        span = pl.ds(chunk * step, step)
+        span = rows_of(chunk)
         return remote(
             pert.at[:, span, :], halo.at[side, :, span, :],
             halo_send.at[side, chunk], halo_recv.at[side, chunk], target,
@@ -74,21 +92,21 @@
     def term_copy(db, dm, chunk, target):
         place = slot(db, dm)
         return remote(
-            term_out.at[db + 1, owned(chunk, lax.rem(m + dm, mem_size)), :],
-            term_in.at[chunk, place],
+            term_out.at[db + 1, *owned(chunk, lax.rem(m + dm, mem_size))],
+            term_in.at[terms_of(chunk, place)],
             term_send.at[chunk, place], term_recv.at[chunk, place], target,
         )
 
     def weight_copy(db, dm, chunk, owner, target):
         place = slot(db, dm)
         return remote(
-            weighted.at[1, owned(chunk, owner), :], weighted.at[1 - db, owned(chunk, owner), :],
+            weighted.at[1, *owned(chunk, owner)], weighted.at[1 - db, *owned(chunk, owner)],
             weight_send.at[chunk, place], weight_recv.at[chunk, place], target,
         )
 
     def inc_copy(dm, chunk, owner, target):
         return remote(
-            total.at[owned(chunk, owner), :], total.at[owned(chunk, owner), :],
+            total.at[owned(chunk, owner)], total.at[owned(chunk, owner)],
             inc_send.at[chunk, dm], inc_recv.at[chunk, dm], target,
         )
 
@@ -120,8 +138,7 @@
             halo[side] = jnp.zeros(halo.shape[1:], halo.dtype)
             weighted[1 + db] = jnp.zeros((rows, cols), weighted.dtype)
             for dm in range(mem_size):
-                for chunk in range(CHUNKS):
-                    term_in[chunk, slot(-db, dm)] = jnp.zeros((part, cols), term_in.dtype)
+                term_in[slot(-db, dm)] = jnp.zeros(term_in.shape[1:], term_in.dtype)
         pl.when(jnp.logical_not(has[db]))(clear)
 
     inner = lax.broadcasted_iota(jnp.int32, (rows, rows), 0).astype(jnp.float32)
@@ -130,6 +147,14 @@
         gap = inner - outer + BAND * (1 - block)
         values = jnp.where(jnp.abs(gap) <= BAND, taper(gap, ROW_SCALE), 0.0)
         row_table[:, block * rows:(block + 1) * rows] = values.astype(jnp.bfloat16)
+    for chunk in range(CHUNKS):
+        size = steps[chunk]
+        inner = lax.broadcasted_iota(jnp.int32, (rows, 3 * size), 0).astype(jnp.float32)
+        outer = lax.broadcasted_iota(jnp.int32, (rows, 3 * size), 1)
+        block = (outer >= size).astype(jnp.int32) + (outer >= 2 * size).astype(jnp.int32)
+        gap = inner - (outer + starts[chunk] - BAND + block * (rows - size)).astype(jnp.float32)
+        values = jnp.where(jnp.abs(gap) <= BAND, taper(gap, ROW_SCALE), 0.0)
+        tables[chunk][...] = values.astype(jnp.bfloat16)
     place = lax.broadcasted_iota(jnp.int32, (cols, cols), 0).astype(jnp.float32)
     other = lax.broadcasted_iota(jnp.int32, (cols, cols), 1).astype(jnp.float32)
     col_table[...] = taper(place - other, COL_SCALE).astype(jnp.bfloat16)
@@ -151,39 +176,45 @@
         for dm in range(1, mem_size):
             term_copy(0, dm, chunk, device(0, dm)).start()
 
-    def send_terms(chunk):
-        for db in (-1, 1):
-            def terms(db=db):
-                side = 0 if db == -1 else 1
-                halo_copy(-db, chunk, device(db, 0)).wait_recv()
-
-                def tile(t, carry):
-                    span = pl.ds(pl.multiple_of(chunk * step + t * TILE, TILE), TILE)
-                    acc = jnp.zeros((TILE, cols), jnp.float32)
-                    for k in range(members):
-                        acc += halo[side, k, span, :].astype(jnp.float32) * local[side, k, span, :]
-                    term_out[db + 1, span, :] = acc.astype(jnp.bfloat16)
-                    return carry
-
-                lax.fori_loop(0, step // TILE, tile, 0)
-                for dm in range(mem_size):
-                    term_copy(db, dm, chunk, device(db, dm)).start()
-            when(db, terms)
+    def send_terms(chunk, db, side):
+        def terms():
+            span = rows_of(chunk)
+            remote(
+                pert.at[:, span, :], halo.at[side, :, span, :],
+                halo_send.at[side, chunk], halo_recv.at[side, chunk], device(db, 0),
+            ).wait_recv()
+
+            def tile(t, carry):
+                span = pl.ds(pl.multiple_of(starts[chunk] + t * TILE, TILE), TILE)
+                acc = jnp.zeros((TILE, cols), jnp.float32)
+                for k in range(members):
+                    acc += halo[side, k, span, :].astype(jnp.float32) * local[side, k, span, :]
+                term_out[db + 1, span, :] = acc.astype(jnp.bfloat16)
+                return carry
+
+            lax.fori_loop(0, steps[chunk] // TILE, tile, 0)
+            for dm in range(mem_size):
+                term_copy(db, dm, chunk, device(db, dm)).start()
+        pl.when(jnp.logical_and(i + db >= 0, i + db < space_size))(terms)
+
+    odd = lax.rem(i, 2)
+    for chunk in range(CHUNKS):
+        send_terms(chunk, 1 - 2 * odd, 1 - odd)
 
     def send_weighted(chunk):
         for db, dm in peers:
             when(-db, lambda db=db, dm=dm: term_copy(db, dm, chunk, device(-db, -dm)).wait_recv())
         span = owned(chunk, m)
-        sums = centre[span, :]
-        for db, dm in peers:
-            sums += term_in[chunk, slot(db, dm)].astype(jnp.float32)
-        total[span, :] = sums
-        weighted[1, span, :] = (
-            own_weight[span, :] * (sums - own_innovation[span, :])
+        sums = centre[span]
+        for db, dm in peers:
+            sums += term_in[terms_of(chunk, slot(db, dm))].astype(jnp.float32)
+        total[span] = sums
+        weighted[1, *span] = (
+            own_weight[span] * (sums - own_innovation[span])
         ).astype(jnp.bfloat16)
         for db, dm in peers:
             when(db, lambda db=db, dm=dm: weight_copy(db, dm, chunk, m, device(db, dm)).start())
-        for dm in range(1, mem_size):
+        for dm in inc_peers:
             inc_copy(dm, chunk, m, device(0, dm)).start()
 
     def adjoint_cols(chunk):
@@ -191,39 +222,42 @@
             owner = lax.rem(m - dm + mem_size, mem_size)
             when(-db, lambda db=db, dm=dm, owner=owner: weight_copy(
                 db, dm, chunk, owner, device(-db, -dm)).wait_recv())
-        span = pl.ds(chunk * step, step)
+        span = rows_of(chunk)
+
+        final = chunk == CHUNKS - 1
 
         def member(k, carry):
             fields = (halo[0, k, span, :], own_pert[k, span, :], halo[1, k, span, :])
             for block, field in enumerate(fields):
                 product = field * weighted[block, span, :]
-                columns[k, pl.ds(block * rows + chunk * step, step), :] = dot(
+                adjoints[chunk][k, block * steps[chunk]:(block + 1) * steps[chunk], :] = dot(
                     product, col_table[...]
                 ).astype(jnp.bfloat16)
+            sums = dot(tables[chunk][...], adjoints[chunk][k])
+            if chunk:
+                sums += accumulated[k]
+            if final:
+                result[k] = sums.astype(jnp.bfloat16)
+                out_copy(k).start()
+            else:
+                accumulated[k] = sums
             return carry
 
-        lax.fori_loop(0, members, member, 0)
+        lax.fori_loop(0, members, member, 0, unroll=UNROLL)
+
+    def out_copy(k):
+        return pltpu.make_async_copy(result.at[k], gradient.at[k], out_sem.at[k])
 
     for turn in range(CHUNKS + 2):
         if turn < CHUNKS:
-            send_terms(turn)
+            send_terms(turn, 2 * odd - 1, odd)
         if 0 <= turn - 1 < CHUNKS:
             send_weighted(turn - 1)
         if 0 <= turn - 2 < CHUNKS:
             adjoint_cols(turn - 2)
 
-    def out_copy(k):
-        return pltpu.make_async_copy(result.at[k], gradient.at[k], out_sem.at[k])
-
-    def last(k, carry):
-        result[k] = dot(row_table[...], columns[k]).astype(jnp.bfloat16)
-        out_copy(k).start()
-        return carry
-
-    lax.fori_loop(0, members, last, 0)
-
-    for chunk in range(CHUNKS):
-        for dm in range(1, mem_size):
+    for chunk in range(CHUNKS):
+        for dm in inc_peers:
             owner = lax.rem(m - dm + mem_size, mem_size)
             inc_copy(dm, chunk, owner, device(0, -dm)).wait_recv()
     if increment.shape[1] == cols:
@@ -241,11 +275,26 @@
                 term_copy(db, dm, chunk, device(db, dm)).wait_send()
                 weight_copy(db, dm, chunk, m, device(db, dm)).wait_send()
             when(db, sent)
-        for dm in range(1, mem_size):
+        for dm in inc_peers:
             inc_copy(dm, chunk, m, device(0, dm)).wait_send()
     for k in range(members):
         out_copy(k).wait()
     inc_out.wait()
+
+
+def deliver(gradient, increment, gradient_out, increment_out, held, held_increment, in_sem, out_sem):
+    members = gradient.shape[0]
+    steps = [(gradient.at[k], held.at[k], gradient_out.at[k]) for k in range(members)]
+    steps.append((increment, held_increment, increment_out))
+    arrivals = [pltpu.make_async_copy(src, mid, in_sem.at[n]) for n, (src, mid, _) in enumerate(steps)]
+    leaves = [pltpu.make_async_copy(mid, dst, out_sem.at[n]) for n, (_, mid, dst) in enumerate(steps)]
+    for copy in arrivals:
+        copy.start()
+    for arrival, leave in zip(arrivals, leaves):
+        arrival.wait()
+        leave.start()
+    for leave in leaves:
+        leave.wait()
 
 
 def on_device(control, perturbations, innovation, error_weight):
@@ -254,7 +303,7 @@
     mem_size = lax.axis_size("mem")
     share = cols // mem_size
     aligned = share % 128 == 0
-    part = rows // CHUNKS // mem_size
+    steps = [rows * size // 8 for size in SIZES]
     slots = 3 * mem_size
     bf16, f32 = jnp.bfloat16, jnp.float32
     dma = pltpu.SemaphoreType.DMA
@@ -264,7 +313,7 @@
             jax.ShapeDtypeStruct((members, rows, cols), bf16),
             jax.ShapeDtypeStruct((rows, share if aligned else cols), f32),
         ),
-        in_specs=[pl.BlockSpec(memory_space=pl.ANY)] * 4,
+        in_specs=[pl.BlockSpec(memory_space=pltpu.HBM)] * 4,
         out_specs=(pl.BlockSpec(memory_space=pl.ANY),) * 2,
         scratch_shapes=[
             pltpu.VMEM((members, rows, cols), bf16),
@@ -275,13 +324,15 @@
             pltpu.VMEM((2, members, rows, cols), f32),
             pltpu.VMEM((rows, cols), f32),
             pltpu.VMEM((3, rows, cols), bf16),
-            pltpu.VMEM((CHUNKS, slots, part, cols), bf16),
+            pltpu.VMEM((slots, rows, share) if aligned else (slots, rows // mem_size, cols), bf16),
             pltpu.VMEM((3, rows, cols), bf16),
             pltpu.VMEM((rows, cols), f32),
-            pltpu.VMEM((members, 3 * rows, cols), bf16),
             pltpu.VMEM((members, rows, cols), bf16),
             pltpu.VMEM((cols, cols), bf16),
             pltpu.VMEM((rows, 3 * rows), bf16),
+            *[pltpu.VMEM((rows, 3 * step), bf16) for step in steps],
+            *[pltpu.VMEM((members, 3 * step, cols), bf16) for step in steps],
+            pltpu.VMEM((members, rows, cols), f32),
             dma((4,)),
             dma((2, CHUNKS)),
             dma((2, CHUNKS)),
@@ -294,12 +345,26 @@
             dma((members,)),
         ],
         compiler_params=pltpu.CompilerParams(
-            collective_id=0, has_side_effects=True, vmem_limit_bytes=40 * 1024 * 1024
+            collective_id=0, has_side_effects=True, vmem_limit_bytes=60 * 1024 * 1024
         ),
     )(control, perturbations, innovation, error_weight)
     if not aligned:
         increment = lax.dynamic_slice_in_dim(increment, lax.axis_index("mem") * share, share, 1)
-    return gradient, increment
+    return pl.pallas_call(
+        deliver,
+        out_shape=(
+            jax.ShapeDtypeStruct((members, rows, cols), bf16),
+            jax.ShapeDtypeStruct((rows, share), f32),
+        ),
+        in_specs=[pl.BlockSpec(memory_space=pl.ANY)] * 2,
+        out_specs=(pl.BlockSpec(memory_space=pl.ANY),) * 2,
+        scratch_shapes=[
+            pltpu.VMEM((members, rows, cols), bf16),
+            pltpu.VMEM((rows, share), f32),
+            dma((members + 1,)),
+            dma((members + 1,)),
+        ],
+    )(gradient, increment)
 
 
 def solution(mesh):

time: 50.2 us -> 43.5 us (0.87)
  local copies, waits for them, and re-layouts: 5.97 us -> 0 us
  Pallas kernels: 43.3 us -> 42.7 us
    unnamed x10 -> x0, local copies, waits for them, and re-layouts: 5.97 us -> none
    pallas_call x1, Pallas kernels: 43.3 us -> 40.6 us  [on_device(): pl.pallas_call(functools.partial(kernel, space_size, mem_size, share), ou...]
    pallas_call x0 -> x1, Pallas kernels: none -> 2.15 us  [on_device(): pl.pallas_call(deliver, out_shape=(jax.ShapeDtypeStruct((members, rows, c...]
where the time goes in v2:
time: 43.5 us; the launch traced here: 43.4 us
  Pallas kernels  42.7 us (98%)
  between operations  0.64 us (1%)
    pallas_call x1, Pallas kernels, on_device(): pl.pallas_call(functools.partial(kernel, space_size, mem_size, share), ou...  40.6 us
    pallas_call x1, Pallas kernels, on_device(): pl.pallas_call(deliver, out_shape=(jax.ShapeDtypeStruct((members, rows, c...  2.15 us

profile of v2, /device:TPU:1, one launch (start us, length us, event | category | flops | bytes accessed | tf_op | source)
XLA Modules:
  0.0 43.4 jit_solution(8757375089154869132)
XLA Ops:
  0.6 40.6 %shard_map.59 = (bf16[8,256,256]{2,1,0:T(8,128)(2,1)}, f32[256,128]{1,0:T(8,128)}) custom-call(bf16[8,256,256]{2,1,0:T(8,128)(2,1)} %control.1, bf16[8,256,256]{2,1,0:T(8,128)(2,1)} %pert.1, f32[256,256]{1,0:T(8,128)} %innovation.1, f32[256,256]{1,0:T(8,128)} %error_weight.1), custom_call_target="tpu_custom_call" | custom-call | tf_op jit(solution)/shard_map/pallas_call | solution.py:310
  41.2 2.1 %shard_map.60 = (bf16[8,256,256]{2,1,0:T(8,128)(2,1)}, f32[256,128]{1,0:T(8,128)}) custom-call(bf16[8,256,256]{2,1,0:T(8,128)(2,1)} %get-tuple-element.4.gradient, f32[256,128]{1,0:T(8,128)} %get-tuple-element.5.increment), custom_call_target="tpu_custom_call" | custom-call | tf_op jit(solution)/shard_map/pallas_call | solution.py:353

commit v3 on v2

--- a/solution.py
+++ b/solution.py
@@ -14,7 +14,7 @@
 SIZES = (4, 4)
 CHUNKS = len(SIZES)
 TILE = 16
-UNROLL = 4
+UNROLL = 8
 MESH = pl.DeviceIdType.MESH
 
 
@@ -128,9 +128,16 @@
     sides = has[-1].astype(jnp.int32) + has[1].astype(jnp.int32)
     pl.semaphore_wait(barrier, mem_size - 1 + mem_size * sides)
 
-    for chunk in range(CHUNKS):
-        for db in (1, -1):
-            when(db, lambda db=db, chunk=chunk: halo_copy(db, chunk, device(db, 0)).start())
+    odd = lax.rem(i, 2)
+    for db, side in ((2 * odd - 1, 1 - odd), (1 - 2 * odd, odd)):
+        for chunk in range(CHUNKS):
+            def send(db=db, side=side, chunk=chunk):
+                span = rows_of(chunk)
+                remote(
+                    pert.at[:, span, :], halo.at[side, :, span, :],
+                    halo_send.at[side, chunk], halo_recv.at[side, chunk], device(db, 0),
+                ).start()
+            pl.when(jnp.logical_and(i + db >= 0, i + db < space_size))(send)
 
     for db in (-1, 1):
         def clear(db=db):
@@ -197,7 +204,6 @@
                 term_copy(db, dm, chunk, device(db, dm)).start()
         pl.when(jnp.logical_and(i + db >= 0, i + db < space_size))(terms)
 
-    odd = lax.rem(i, 2)
     for chunk in range(CHUNKS):
         send_terms(chunk, 1 - 2 * odd, 1 - odd)
 

time: 43.5 us -> 43.2 us (level)
    pallas_call x1, Pallas kernels: 40.6 us -> 40.1 us  [on_device(): pl.pallas_call(functools.partial(kernel, space_size, mem_size, share), ou...]
where the time goes in v3:
time: 43.2 us; the launch traced here: 42.9 us
  Pallas kernels  42.3 us (98%)
  between operations  0.64 us (1%)
    pallas_call x1, Pallas kernels, on_device(): pl.pallas_call(functools.partial(kernel, space_size, mem_size, share), ou...  40.1 us
    pallas_call x1, Pallas kernels, on_device(): pl.pallas_call(deliver, out_shape=(jax.ShapeDtypeStruct((members, rows, c...  2.15 us

profile of v3, /device:TPU:1, one launch (start us, length us, event | category | flops | bytes accessed | tf_op | source)
XLA Modules:
  0.0 42.9 jit_solution(14890593217152993738)
XLA Ops:
  0.6 40.1 %shard_map.59 = (bf16[8,256,256]{2,1,0:T(8,128)(2,1)}, f32[256,128]{1,0:T(8,128)}) custom-call(bf16[8,256,256]{2,1,0:T(8,128)(2,1)} %control.1, bf16[8,256,256]{2,1,0:T(8,128)(2,1)} %pert.1, f32[256,256]{1,0:T(8,128)} %innovation.1, f32[256,256]{1,0:T(8,128)} %error_weight.1), custom_call_target="tpu_custom_call" | custom-call | tf_op jit(solution)/shard_map/pallas_call | solution.py:316
  40.8 2.1 %shard_map.60 = (bf16[8,256,256]{2,1,0:T(8,128)(2,1)}, f32[256,128]{1,0:T(8,128)}) custom-call(bf16[8,256,256]{2,1,0:T(8,128)(2,1)} %get-tuple-element.4.gradient, f32[256,128]{1,0:T(8,128)} %get-tuple-element.5.increment), custom_call_target="tpu_custom_call" | custom-call | tf_op jit(solution)/shard_map/pallas_call | solution.py:359
